TPU v7x, 128 devices: a whole 4x4x4 slice. The times are simulated.
128 devices in a mesh: row: 8 (over x, y_hi), col: 16 (over z, y_lo, core).
Axes of the slice: x: 4, y: 4 (y_hi: 2, y_lo: 2; y = y_hi * 2 + y_lo), z: 4, core: 2. Of those that a mesh axis runs over, the one named last changes fastest.
Arguments:
- density: float32 [5120, 5120], P('row', 'col'), as said below
- pattern: int32 [80, 80], P('row', 'col'), may hold values from 0 to 1, as said below
- weights: float32 [5120], P('row'), may hold values from 0.5 to 5
Outputs:
- purified: float32 [5120, 5120], P('row', 'col')
- checks: float32 [2, 5120], P(None, 'col')
Inputs may be any that keep to these rules, and one draw needn't show every extreme that they name: pattern is symmetric, and every block with |a - b| <= 2 is nonzero; the number of nonzero blocks differs strongly between block rows. density is symmetric and zero outside the blocks that pattern marks.
All inputs are finite; a program needn't handle non-finite values.
Results may differ from a plain program's by a relative error of at most 0.00012.
Values sent between devices are 32-bit elements; how exact they have to be, the bound alone decides.
A program may use at most 64 MiB of HBM per device.

v0:
```python
import jax
import jax.numpy as jnp
from jax import lax
from jax.sharding import PartitionSpec as P

BLK = 64


def full_dot(first, second):
    return jnp.dot(
        first, second, precision=lax.Precision.HIGHEST, preferred_element_type=jnp.float32
    )


def expand_mask(pattern):
    return jnp.repeat(jnp.repeat(pattern.astype(jnp.float32), BLK, axis=0), BLK, axis=1)


def multiply(left_tile, column, weight_row):
    partial_row = full_dot(weight_row, left_tile)
    result = full_dot(lax.all_gather(left_tile, "col", axis=1, tiled=True), column)
    summed = lax.psum(partial_row, "row")
    full_check = lax.all_gather(summed, "col", axis=1, tiled=True)
    check_row = full_dot(full_check, column)
    return (result, check_row)


def body(density, pattern, weights):
    block_mask = expand_mask(pattern)
    current = density
    weight_row = weights[None, :]
    checks = []
    column = lax.all_gather(current, "row", axis=0, tiled=True)
    square, first_check = multiply(current, column, weight_row)
    square = block_mask * square
    cube_term, second_check = multiply(square, column, weight_row)
    cube_term = block_mask * cube_term
    current = 3.0 * square - 2.0 * cube_term
    checks.append(first_check)
    checks.append(second_check)
    return (current, jnp.concatenate(checks, axis=0))


def solution(mesh):
    in_specs = (P("row", "col"), P("row", "col"), P("row"))
    out_specs = (P("row", "col"), P(None, "col"))
    return jax.shard_map(body, mesh=mesh, in_specs=in_specs, out_specs=out_specs, check_vma=False)
```

profile of v0, /device:TPU:0, one launch (start us, length us, event | category | flops | bytes accessed | tf_op | source)
XLA Modules:
  0.0 325.3 jit_solution(1333417447258999586)
XLA Ops:
  7.2 0.0 all-gather.6.cloned.1.call-start
  7.2 0.7 all-gather.6.cloned.1.call-update
  7.9 0.0 all-gather.4.cloned.1.call-start
  7.9 0.7 all-gather.4.cloned.1.call-update
  8.6 0.0 all-gather.8.cloned.1.call-start
  8.7 0.7 convert_element_type.3
  9.4 0.1 broadcast_in_dim.7
  9.5 0.1 reshape.24
  9.5 94.3 %all-gather.6.cloned.1.call-done = f32[5120,320]{0,1:T(8,128)} async-done(((f32[640,320]{0,1:T(8,128)}), f32[5120,320]{0,1:T(8,128)}) %all-gather.6.cloned.1.call-update) | async-done | bytes 6553616 | tf_op jit(solution)/shard_map/all_gather | solution.py:33
  103.9 73.9 %all-gather.4.cloned.1.call-done = f32[640,5120]{0,1:T(8,128)} async-done(((f32[640,320]{0,1:T(8,128)}), f32[640,5120]{0,1:T(8,128)}) %all-gather.4.cloned.1.call-update) | async-done | bytes 13107216 | tf_op jit(solution)/shard_map/all_gather | solution.py:21
  177.8 0.1 broadcast_in_dim.8
  177.9 0.0 copy-start.2
  177.9 0.0 copy-start.3
  177.9 0.0 copy-start.1
  177.9 20.3 %convolution_multiply_fusion.1 = f32[640,320]{0,1:T(8,128)} fusion(f32[640,320]{0,1:T(8,128)S(1)} %bitcast.18, f32[640,5120]{0,1:T(8,128)} %all-gather.4.cloned.1.call-done, f32[5120,320]{0,1:T(8,128)} %all-gather.6.cloned.1.call-done), kind=kOutput, calls=%fused_computation.1 | convolution fusion | flops 12583116800 | bytes 21299200 | tf_op jit(solution)/shard_map/dot_general | solution.py:10
  198.2 0.0 all-gather.8.cloned.1.call-update
  198.3 0.0 copy-done.2
  198.3 0.0 copy-done.3
  198.3 0.6 dynamic-slice
  199.5 0.0 copy-done.1
  199.5 0.8 fusion.2
  200.3 2.0 fusion.4
  202.3 24.4 %all-reduce.3 = (f32[1,320]{1,0:T(1,128)S(1)}, f32[1,320]{1,0:T(1,128)S(1)}) all-reduce(f32[1,320]{1,0:T(1,128)S(1)} %fusion.4, f32[1,320]{1,0:T(1,128)S(1)} %fusion.2), channel_id=1, replica_groups=mesh['row'=8,'col'=16] {'row'}, use_global_device_ids=true, to_apply=%region_1.0 | all-reduce | flops 640 | bytes 5120 | tf_op jit(solution)/shard_map/psum | solution.py:22
  226.7 0.3 dynamic-update-slice
  227.0 0.3 dynamic-update-slice.1
  227.3 55.8 %all-reduce.2 = (f32[5120]{0:T(1024)S(1)}, f32[5120]{0:T(1024)S(1)}) all-reduce(f32[5120]{0:T(1024)S(1)} %dynamic-update-slice.1, f32[5120]{0:T(1024)S(1)} %dynamic-update-slice), channel_id=1, replica_groups=mesh['row'=8,'col'=16] {'col'}, use_global_device_ids=true, to_apply=%add.1 | all-reduce | flops 10240 | bytes 81920 | tf_op jit(solution)/shard_map/reshape.10
  283.1 0.0 copy-start
  283.1 7.4 %fusion.3 = f32[1,320]{1,0:T(1,128)S(1)} fusion(f32[5120,1]{0,1:T(1,128)S(1)} %bitcast.21, f32[5120,320]{0,1:T(8,128)} %all-gather.6.cloned.1.call-done), kind=kOutput, calls=%fused_computation.6 | convolution fusion | flops 19660800 | bytes 6575360 | tf_op jit(solution)/shard_map/dot_general | solution.py:10
  290.5 7.3 %fusion.5 = f32[1,320]{1,0:T(1,128)S(1)} fusion(f32[5120,1]{0,1:T(1,128)S(1)} %bitcast.20, f32[5120,320]{0,1:T(8,128)} %all-gather.6.cloned.1.call-done), kind=kOutput, calls=%fused_computation.8 | convolution fusion | flops 19660800 | bytes 6575360 | tf_op jit(solution)/shard_map/dot_general | solution.py:10
  297.8 0.6 pad_maximum_fusion
  298.4 0.0 all-gather.8.cloned.1.call-done
  298.4 0.0 copy-done
  298.4 20.3 %fusion.1 = f32[640,320]{0,1:T(8,128)} fusion(f32[640,320]{0,1:T(8,128)S(1)} %bitcast.19, f32[640,5120]{0,1:T(8,128)} %all-gather.8.cloned.1.call-done, f32[5120,320]{0,1:T(8,128)} %all-gather.6.cloned.1.call-done, f32[640,320]{0,1:T(8,128)S(1)} %copy-done), kind=kOutput, calls=%fused_computation.3 | convolution fusion | flops 12583731200 | bytes 22118400 | tf_op jit(solution)/shard_map/dot_general | solution.py:10
  (5 shorter events, 0.1 us)
Async XLA Ops:
  7.2 96.7 %all-gather.6.cloned.1.call-start = ((), (), s32[]{:S(2)}) async-start(), calls=%async_computation.1 | async-start | bytes 7372800 | tf_op jit(solution)/shard_map/all_gather | solution.py:33
  7.9 169.9 %all-gather.4.cloned.1.call-start = ((), (), s32[]{:S(2)}) async-start(), calls=%async_computation | async-start | bytes 13926400 | tf_op jit(solution)/shard_map/all_gather | solution.py:21
  8.6 289.8 %all-gather.8.cloned.1.call-start = ((), (), s32[]{:S(2)}) async-start(), calls=%async_computation.2 | async-start | bytes 13926400 | tf_op jit(solution)/shard_map/all_gather | solution.py:21
  177.9 20.4 %copy-start.2 = (f32[640]{0:T(1024)S(1)}, f32[640]{0:T(1024)}, u32[]{:S(2)}) copy-start(f32[640]{0:T(1024)} %param.5) | copy-start | bytes 7684
  177.9 20.4 %copy-start.3 = (u32[128]{0:T(128)S(1)}, u32[128]{0:T(128)}, u32[]{:S(2)}) copy-start(u32[128]{0:T(128)} %constant.7) | copy-start | bytes 1540
  177.9 21.7 %copy-start.1 = (f32[640,320]{0,1:T(8,128)S(1)}, f32[640,320]{0,1:T(8,128)}, u32[]{:S(2)}) copy-start(f32[640,320]{0,1:T(8,128)} %param.3) | copy-start | bytes 2457604
  283.1 15.4 %copy-start = (f32[640,320]{0,1:T(8,128)S(1)}, f32[640,320]{0,1:T(8,128)}, u32[]{:S(2)}) copy-start(f32[640,320]{0,1:T(8,128)} %convolution_multiply_fusion.1) | copy-start | bytes 2457604
Sparse Core Ops, SparseCore 0:
  10.3 93.5 all-gather.5
  105.6 72.1 all-gather.3
  198.4 76.7 all-gather.7
where the time goes:
time: 325 us
  waiting for transfers between devices  170 us (52%)
  blocking collectives  80.2 us (25%)
  matrix products  58.1 us (18%)
  between operations  14.5 us (4%)
    all_gather x1, waiting for transfers between devices, body(): column = lax.all_gather(current, 'row', axis=0, tiled=True)  94.3 us
    all_gather x2, waiting for transfers between devices, multiply(): lax.all_gather(left_tile, 'col', axis=1, tiled=True)  73.9 us
    dot_general x6, matrix products, full_dot(): jnp.dot(first, second, precision=lax.Precision.HIGHEST, preferred_element...  58.1 us
    another operation x1, blocking collectives  55.8 us
    psum x1, blocking collectives, multiply(): summed = lax.psum(partial_row, 'row')  24.4 us
  transfers between devices with their start and end apart: 3, of which 2 were waited for; matrix products, arithmetic and copies ran while one was open for 6% of the time, Pallas kernels for 0%

commit v1 on v0

--- a/solution.py
+++ b/solution.py
@@ -19,7 +19,7 @@
 def multiply(left_tile, column, weight_row):
     partial_row = full_dot(weight_row, left_tile)
     result = full_dot(lax.all_gather(left_tile, "col", axis=1, tiled=True), column)
-    summed = lax.psum(partial_row, "row")
+    summed = jnp.sum(lax.all_gather(partial_row, "row"), 0)
     full_check = lax.all_gather(summed, "col", axis=1, tiled=True)
     check_row = full_dot(full_check, column)
     return (result, check_row)

time: 325 us -> 344 us (1.058)
  blocking collectives: 80.2 us -> 97 us
    unnamed x0 -> x2, blocking collectives: none -> 97 us
    another operation x1 -> x0, blocking collectives: 55.8 us -> none
    psum x1 -> x0, blocking collectives: 24.4 us -> none  [multiply(): summed = lax.psum(partial_row, 'row')]
where the time goes in v1:
time: 344 us
  waiting for transfers between devices  170 us (49%)
  blocking collectives  97 us (28%)
  matrix products  58.1 us (17%)
  between operations  15.1 us (4%)
    unnamed x2, blocking collectives  97 us
    all_gather x1, waiting for transfers between devices, body(): column = lax.all_gather(current, 'row', axis=0, tiled=True)  94.3 us
    all_gather x2, waiting for transfers between devices, multiply(): lax.all_gather(left_tile, 'col', axis=1, tiled=True)  73.9 us
    dot_general x6, matrix products, full_dot(): jnp.dot(first, second, precision=lax.Precision.HIGHEST, preferred_element...  58.1 us
  transfers between devices with their start and end apart: 3, of which 2 were waited for; matrix products, arithmetic and copies ran while one was open for 6% of the time, Pallas kernels for 0%

profile of v1, /device:TPU:0, one launch (start us, length us, event | category | flops | bytes accessed | tf_op | source)
XLA Modules:
  0.0 344.0 jit_solution(11855431686685615197)
XLA Ops:
  7.2 0.0 all-gather.10.cloned.1.call-start
  7.2 0.7 all-gather.10.cloned.1.call-update
  7.9 0.0 all-gather.8.cloned.1.call-start
  7.9 0.7 all-gather.8.cloned.1.call-update
  8.6 0.0 all-gather.12.cloned.1.call-start
  8.7 0.7 convert_element_type.3
  9.4 0.1 broadcast_in_dim.7
  9.5 0.1 reshape.28
  9.5 94.3 %all-gather.10.cloned.1.call-done = f32[5120,320]{0,1:T(8,128)} async-done(((f32[640,320]{0,1:T(8,128)}), f32[5120,320]{0,1:T(8,128)}) %all-gather.10.cloned.1.call-update) | async-done | bytes 6553616 | tf_op jit(solution)/shard_map/all_gather | solution.py:33
  103.9 73.9 %all-gather.8.cloned.1.call-done = f32[640,5120]{0,1:T(8,128)} async-done(((f32[640,320]{0,1:T(8,128)}), f32[640,5120]{0,1:T(8,128)}) %all-gather.8.cloned.1.call-update) | async-done | bytes 13107216 | tf_op jit(solution)/shard_map/all_gather | solution.py:21
  177.8 0.1 broadcast_in_dim.8
  177.9 0.0 copy-start.2
  177.9 0.0 copy-start.4
  177.9 0.0 copy-start.3
  177.9 0.0 copy-start.1
  177.9 20.3 %convolution_multiply_fusion.1 = f32[640,320]{0,1:T(8,128)} fusion(f32[640,320]{0,1:T(8,128)S(1)} %bitcast.19, f32[640,5120]{0,1:T(8,128)} %all-gather.8.cloned.1.call-done, f32[5120,320]{0,1:T(8,128)} %all-gather.10.cloned.1.call-done), kind=kOutput, calls=%fused_computation.1 | convolution fusion | flops 12583116800 | bytes 21299200 | tf_op jit(solution)/shard_map/dot_general | solution.py:10
  198.2 0.0 all-gather.12.cloned.1.call-update
  198.3 0.0 copy-done.2
  198.3 0.0 copy-done.4
  198.3 0.6 dynamic-slice
  198.9 0.0 copy-done.3
  198.9 0.6 dynamic-slice.1
  200.7 0.0 copy-done.1
  200.7 0.8 convolution_reduce_fusion.1
  201.5 0.3 dynamic-update-slice
  201.8 1.9 convolution_reduce_fusion
  203.8 0.3 dynamic-update-slice.2
  204.0 42.3 %all-reduce.5 = (f32[2560]{0:T(1024)S(1)}, f32[2560]{0:T(1024)S(1)}) all-reduce(f32[2560]{0:T(1024)S(1)} %dynamic-update-slice.2, f32[2560]{0:T(1024)S(1)} %dynamic-update-slice), channel_id=4, replica_groups=mesh['row'=8,'col'=16] {'row'}, use_global_device_ids=true, to_apply=%add.2 | all-reduce | flops 5120 | bytes 40960
  246.3 0.1 reshape.32
  246.4 0.1 reshape.34
  246.5 0.3 dynamic-update-slice.1
  246.8 0.3 dynamic-update-slice.3
  247.1 54.7 %all-reduce.4 = (f32[5120]{0:T(1024)S(1)}, f32[5120]{0:T(1024)S(1)}) all-reduce(f32[5120]{0:T(1024)S(1)} %dynamic-update-slice.3, f32[5120]{0:T(1024)S(1)} %dynamic-update-slice.1), channel_id=5, replica_groups=mesh['row'=8,'col'=16] {'col'}, use_global_device_ids=true, to_apply=%add.3 | all-reduce | flops 10240 | bytes 81920
  301.8 0.0 copy-start
  301.8 7.4 %fusion.2 = f32[1,320]{1,0:T(1,128)S(1)} fusion(f32[5120,1]{0,1:T(1,128)S(1)} %bitcast.22, f32[5120,320]{0,1:T(8,128)} %all-gather.10.cloned.1.call-done), kind=kOutput, calls=%fused_computation.7 | convolution fusion | flops 19660800 | bytes 6575360 | tf_op jit(solution)/shard_map/dot_general | solution.py:10
  309.2 7.3 %fusion.3 = f32[1,320]{1,0:T(1,128)S(1)} fusion(f32[5120,1]{0,1:T(1,128)S(1)} %bitcast.21, f32[5120,320]{0,1:T(8,128)} %all-gather.10.cloned.1.call-done), kind=kOutput, calls=%fused_computation.8 | convolution fusion | flops 19660800 | bytes 6575360 | tf_op jit(solution)/shard_map/dot_general | solution.py:10
  316.5 0.6 pad_maximum_fusion
  317.1 0.0 all-gather.12.cloned.1.call-done
  317.2 0.0 copy-done
  317.2 20.3 %fusion.1 = f32[640,320]{0,1:T(8,128)} fusion(f32[640,320]{0,1:T(8,128)S(1)} %bitcast.20, f32[640,5120]{0,1:T(8,128)} %all-gather.12.cloned.1.call-done, f32[5120,320]{0,1:T(8,128)} %all-gather.10.cloned.1.call-done, f32[640,320]{0,1:T(8,128)S(1)} %copy-done), kind=kOutput, calls=%fused_computation.3 | convolution fusion | flops 12583731200 | bytes 22118400 | tf_op jit(solution)/shard_map/dot_general | solution.py:10
  (7 shorter events, 0.1 us)
Async XLA Ops:
  7.2 96.7 %all-gather.10.cloned.1.call-start = ((), (), s32[]{:S(2)}) async-start(), calls=%async_computation.1 | async-start | bytes 7372800 | tf_op jit(solution)/shard_map/all_gather | solution.py:33
  7.9 169.9 %all-gather.8.cloned.1.call-start = ((), (), s32[]{:S(2)}) async-start(), calls=%async_computation | async-start | bytes 13926400 | tf_op jit(solution)/shard_map/all_gather | solution.py:21
  8.6 308.5 %all-gather.12.cloned.1.call-start = ((), (), s32[]{:S(2)}) async-start(), calls=%async_computation.2 | async-start | bytes 13926400 | tf_op jit(solution)/shard_map/all_gather | solution.py:21
  177.9 20.4 %copy-start.2 = (f32[640]{0:T(1024)S(1)}, f32[640]{0:T(1024)}, u32[]{:S(2)}) copy-start(f32[640]{0:T(1024)} %param.5) | copy-start | bytes 7684
  177.9 20.4 %copy-start.4 = (u32[128]{0:T(128)S(1)}, u32[128]{0:T(128)}, u32[]{:S(2)}) copy-start(u32[128]{0:T(128)} %constant.9) | copy-start | bytes 1540
  177.9 21.0 %copy-start.3 = (u32[128]{0:T(128)S(1)}, u32[128]{0:T(128)}, u32[]{:S(2)}) copy-start(u32[128]{0:T(128)} %constant.14) | copy-start | bytes 1540
  177.9 22.8 %copy-start.1 = (f32[640,320]{0,1:T(8,128)S(1)}, f32[640,320]{0,1:T(8,128)}, u32[]{:S(2)}) copy-start(f32[640,320]{0,1:T(8,128)} %param.3) | copy-start | bytes 2457604
  301.8 15.4 %copy-start = (f32[640,320]{0,1:T(8,128)S(1)}, f32[640,320]{0,1:T(8,128)}, u32[]{:S(2)}) copy-start(f32[640,320]{0,1:T(8,128)} %convolution_multiply_fusion.1) | copy-start | bytes 2457604
Sparse Core Ops, SparseCore 0:
  10.3 93.5 all-gather.9
  105.6 72.1 all-gather.7
  198.4 76.9 all-gather.11

commit v2 on v0

--- a/solution.py
+++ b/solution.py
@@ -1,9 +1,22 @@
+import functools
 import jax
 import jax.numpy as jnp
 from jax import lax
 from jax.sharding import PartitionSpec as P
 
 BLK = 64
+
+
+def groups_try_all(u_in, net_axis):
+    return jnp.concatenate(
+        lax.all_to_all(
+            jnp.stack(tuple((u_in for _ in range(lax.psum(1, net_axis)))), axis=0), net_axis, 0, 0
+        ),
+        axis=0,
+    )
+
+
+_keep_up_trails = functools.partial(groups_try_all, net_axis="row")
 
 
 def full_dot(first, second):
@@ -30,7 +43,7 @@
     current = density
     weight_row = weights[None, :]
     checks = []
-    column = lax.all_gather(current, "row", axis=0, tiled=True)
+    column = _keep_up_trails(current)
     square, first_check = multiply(current, column, weight_row)
     square = block_mask * square
     cube_term, second_check = multiply(square, column, weight_row)

time: 325 us -> 303 us (0.932)
  waiting for transfers between devices: 170 us -> 129 us
  local copies, waits for them, and re-layouts: 1.36 us -> 12.1 us
  starting transfers between devices: 0.11 us -> 7.25 us
    all_gather x1 -> x0, waiting for transfers between devices: 94.3 us -> none  [body(): column = lax.all_gather(current, 'row', axis=0, tiled=True)]
    all_to_all x0 -> x1, waiting for transfers between devices: none -> 91.3 us  [groups_try_all(): lax.all_to_all(jnp.stack(tuple((u_in for _ in range(lax.psum(1, net_axis)...]
    all_gather x2, waiting for transfers between devices: 73.9 us -> 36.6 us  [multiply(): lax.all_gather(left_tile, 'col', axis=1, tiled=True)]
    all_to_all x0 -> x1, starting transfers between devices: none -> 7.17 us  [groups_try_all(): lax.all_to_all(jnp.stack(tuple((u_in for _ in range(lax.psum(1, net_axis)...]
    reshape x0 -> x1, local copies, waits for them, and re-layouts: none -> 6.5 us  [groups_try_all(): jnp.concatenate(lax.all_to_all(jnp.stack(tuple((u_in for _ in range(lax.p...]
    another operation x0 -> x1, local copies, waits for them, and re-layouts: none -> 4.24 us  [groups_try_all(): jnp.stack(tuple((u_in for _ in range(lax.psum(1, net_axis)))), axis=0)]
  transfers between devices with their start and end apart: 3 -> 3, of which waited for: 2 -> 2; matrix products, arithmetic and copies ran while one was open for 6% -> 10% of each run, Pallas kernels for 0% -> 0%
where the time goes in v2:
time: 303 us
  waiting for transfers between devices  129 us (43%)
  blocking collectives  81.3 us (27%)
  matrix products  58 us (19%)
  between operations  14.8 us (5%)
  local copies, waits for them, and re-layouts  12.1 us (4%)
  starting transfers between devices  7.25 us (2%)
    all_to_all x1, waiting for transfers between devices, groups_try_all(): lax.all_to_all(jnp.stack(tuple((u_in for _ in range(lax.psum(1, net_axis)...  91.3 us
    dot_general x6, matrix products, full_dot(): jnp.dot(first, second, precision=lax.Precision.HIGHEST, preferred_element...  58 us
    another operation x1, blocking collectives  56.1 us
    all_gather x2, waiting for transfers between devices, multiply(): lax.all_gather(left_tile, 'col', axis=1, tiled=True)  36.6 us
    psum x1, blocking collectives, multiply(): summed = lax.psum(partial_row, 'row')  25.2 us
    all_to_all x1, starting transfers between devices, groups_try_all(): lax.all_to_all(jnp.stack(tuple((u_in for _ in range(lax.psum(1, net_axis)...  7.17 us
    reshape x1, local copies, waits for them, and re-layouts, groups_try_all(): jnp.concatenate(lax.all_to_all(jnp.stack(tuple((u_in for _ in range(lax.p...  6.5 us
  transfers between devices with their start and end apart: 3, of which 2 were waited for; matrix products, arithmetic and copies ran while one was open for 10% of the time, Pallas kernels for 0%

profile of v2, /device:TPU:0, one launch (start us, length us, event | category | flops | bytes accessed | tf_op | source)
XLA Modules:
  0.0 302.7 jit_solution(17070025526826073002)
XLA Ops:
  7.2 0.0 all-gather.3.cloned.1.call-start
  7.2 0.7 all-gather.3.cloned.1.call-update
  7.9 4.2 %stack.2 = f32[8,640,320]{1,2,0:T(8,128)} broadcast(f32[640,320]{0,1:T(8,128)} %param.3), dimensions={1,2} | broadcast | bytes 7372800 | tf_op jit(solution)/shard_map/stack | solution.py:13
  12.1 0.0 copy-start.2
  12.1 7.2 %all-to-all-start = ((f32[8,640,320]{1,2,0:T(8,128)}), f32[8,640,320]{1,2,0:T(8,128)}, u32[]{:S(2)}, u32[]{:S(2)}) async-start(f32[8,640,320]{1,2,0:T(8,128)} %stack.2), calls=%async_computation | async-start | bytes 13107200 | tf_op jit(solution)/shard_map/all_to_all | solution.py:12
  19.3 0.0 all-gather.5.cloned.1.call-start
  19.4 0.0 copy-done.2
  19.4 0.1 broadcast_in_dim.7
  19.5 0.1 reshape.29
  19.5 91.3 %all-to-all-done = f32[8,640,320]{1,2,0:T(8,128)} async-done(((f32[8,640,320]{1,2,0:T(8,128)}), f32[8,640,320]{1,2,0:T(8,128)}, u32[]{:S(2)}, u32[]{:S(2)}) %all-to-all-start) | async-done | bytes 6553632 | tf_op jit(solution)/shard_map/all_to_all | solution.py:12
  110.8 6.5 %copy.7 = f32[8,40,8,640]{3,2,0,1:T(8,128)} copy(f32[8,40,8,640]{3,2,1,0:T(8,128)} %bitcast.4) | data formatting | bytes 13107200 | tf_op jit(solution)/shard_map/reshape | solution.py:11
  117.3 36.6 %all-gather.3.cloned.1.call-done = f32[640,5120]{0,1:T(8,128)} async-done(((f32[640,320]{0,1:T(8,128)}), f32[640,5120]{0,1:T(8,128)}) %all-gather.3.cloned.1.call-update) | async-done | bytes 13107216 | tf_op jit(solution)/shard_map/all_gather | solution.py:34
  153.9 0.1 broadcast_in_dim.8
  154.0 0.0 copy-start.3
  154.0 0.0 copy-start.4
  154.0 0.0 copy-start.1
  154.0 20.3 %convolution_multiply_fusion.1 = f32[640,320]{0,1:T(8,128)} fusion(f32[640,320]{0,1:T(8,128)S(1)} %bitcast.24, f32[640,5120]{0,1:T(8,128)} %all-gather.3.cloned.1.call-done, f32[5120,320]{0,1:T(8,128)} %bitcast.20), kind=kOutput, calls=%fused_computation.1 | convolution fusion | flops 12583116800 | bytes 21299200 | tf_op jit(solution)/shard_map/dot_general | solution.py:23
  174.3 0.0 all-gather.5.cloned.1.call-update
  174.4 0.0 copy-done.3
  174.4 0.0 copy-done.4
  174.4 0.6 dynamic-slice
  175.6 0.0 copy-done.1
  175.6 0.8 fusion.2
  176.5 1.9 fusion.4
  178.3 25.2 %all-reduce.3 = (f32[1,320]{1,0:T(1,128)S(1)}, f32[1,320]{1,0:T(1,128)S(1)}) all-reduce(f32[1,320]{1,0:T(1,128)S(1)} %fusion.4, f32[1,320]{1,0:T(1,128)S(1)} %fusion.2), channel_id=1, replica_groups=mesh['row'=8,'col'=16] {'row'}, use_global_device_ids=true, to_apply=%region_1.0 | all-reduce | flops 640 | bytes 5120 | tf_op jit(solution)/shard_map/psum | solution.py:35
  203.6 0.3 dynamic-update-slice
  203.8 0.3 dynamic-update-slice.1
  204.1 56.1 %all-reduce.2 = (f32[5120]{0:T(1024)S(1)}, f32[5120]{0:T(1024)S(1)}) all-reduce(f32[5120]{0:T(1024)S(1)} %dynamic-update-slice.1, f32[5120]{0:T(1024)S(1)} %dynamic-update-slice), channel_id=1, replica_groups=mesh['row'=8,'col'=16] {'col'}, use_global_device_ids=true, to_apply=%add.1 | all-reduce | flops 10240 | bytes 81920 | tf_op jit(solution)/shard_map/reshape.12
  260.2 0.0 copy-start
  260.2 7.4 %fusion.3 = f32[1,320]{1,0:T(1,128)S(1)} fusion(f32[5120,1]{0,1:T(1,128)S(1)} %bitcast.27, f32[5120,320]{0,1:T(8,128)} %bitcast.21), kind=kOutput, calls=%fused_computation.6 | convolution fusion | flops 19660800 | bytes 6575360 | tf_op jit(solution)/shard_map/dot_general | solution.py:23
  267.6 7.3 %fusion.5 = f32[1,320]{1,0:T(1,128)S(1)} fusion(f32[5120,1]{0,1:T(1,128)S(1)} %bitcast.26, f32[5120,320]{0,1:T(8,128)} %bitcast.22), kind=kOutput, calls=%fused_computation.8 | convolution fusion | flops 19660800 | bytes 6575360 | tf_op jit(solution)/shard_map/dot_general | solution.py:23
  274.9 0.6 pad_maximum_fusion
  275.6 0.0 all-gather.5.cloned.1.call-done
  275.6 0.0 copy-done
  275.6 20.3 %fusion.1 = f32[640,320]{0,1:T(8,128)} fusion(f32[640,320]{0,1:T(8,128)S(1)} %bitcast.25, f32[640,5120]{0,1:T(8,128)} %all-gather.5.cloned.1.call-done, f32[5120,320]{0,1:T(8,128)} %bitcast.23, f32[640,320]{0,1:T(8,128)S(1)} %copy-done), kind=kOutput, calls=%fused_computation.3 | convolution fusion | flops 12583731200 | bytes 22118400 | tf_op jit(solution)/shard_map/dot_general | solution.py:23
  (6 shorter events, 0.1 us)
Async XLA Ops:
  7.2 146.7 %all-gather.3.cloned.1.call-start = ((), (), s32[]{:S(2)}) async-start(), calls=%async_computation.1 | async-start | bytes 13926400 | tf_op jit(solution)/shard_map/all_gather | solution.py:34
  12.1 7.2 %copy-start.2 = (s32[10,5]{0,1:T(8,128)S(1)}, s32[10,5]{0,1:T(8,128)}, u32[]{:S(2)}) copy-start(s32[10,5]{0,1:T(8,128)} %param.4) | copy-start | bytes 604
  12.1 98.7 %all-to-all-start = ((f32[8,640,320]{1,2,0:T(8,128)}), f32[8,640,320]{1,2,0:T(8,128)}, u32[]{:S(2)}, u32[]{:S(2)}) async-start(f32[8,640,320]{1,2,0:T(8,128)} %stack.2), calls=%async_computation | async-start | bytes 13107200 | tf_op jit(solution)/shard_map/all_to_all | solution.py:12
  19.3 256.2 %all-gather.5.cloned.1.call-start = ((), (), s32[]{:S(2)}) async-start(), calls=%async_computation.2 | async-start | bytes 13926400 | tf_op jit(solution)/shard_map/all_gather | solution.py:34
  154.0 20.4 %copy-start.3 = (f32[640]{0:T(1024)S(1)}, f32[640]{0:T(1024)}, u32[]{:S(2)}) copy-start(f32[640]{0:T(1024)} %param.5) | copy-start | bytes 7684
  154.0 20.4 %copy-start.4 = (u32[128]{0:T(128)S(1)}, u32[128]{0:T(128)}, u32[]{:S(2)}) copy-start(u32[128]{0:T(128)} %constant.7) | copy-start | bytes 1540
  154.0 21.6 %copy-start.1 = (f32[640,320]{0,1:T(8,128)S(1)}, f32[640,320]{0,1:T(8,128)}, u32[]{:S(2)}) copy-start(f32[640,320]{0,1:T(8,128)} %param.3) | copy-start | bytes 2457604
  260.2 15.4 %copy-start = (f32[640,320]{0,1:T(8,128)S(1)}, f32[640,320]{0,1:T(8,128)}, u32[]{:S(2)}) copy-start(f32[640,320]{0,1:T(8,128)} %convolution_multiply_fusion.1) | copy-start | bytes 2457604
Sparse Core Ops, SparseCore 0:
  9.7 144.1 all-gather.2
  174.5 78.8 all-gather.4
